TPU v7x, 256 devices: a whole 4x4x8 slice. The times are simulated.
256 devices in a mesh: seq: 32 (over y, z), tensor: 8 (over x, core).
Axes of the slice: x: 4, y: 4, z: 8, core: 2. Of those that a mesh axis runs over, the one named last changes fastest.
Arguments:
- tokens: int32 [4, 128], replicated, may hold values from 0 to 50175
- lengths: int32 [128], replicated, may hold values from 64 to 3072, as said below
- page_table: int32 [128, 24], replicated, may hold values from -1 to 767, as said below
- embedding: bfloat16 [50176, 2048], P('seq', 'tensor'), may hold values from -24 to 24
- ln1_gain: float32 [2048], replicated, may hold values from 0.5 to 1.5
- ln1_bias: float32 [2048], replicated, may hold values from -3 to 3
- w_query: bfloat16 [2048, 2048], P(None, 'tensor'), may hold values from -0.125 to 0.125
- q_bias: float32 [2048], P('tensor'), may hold values from -3 to 3
- w_key: bfloat16 [2048, 2048], P(None, 'tensor'), may hold values from -0.125 to 0.125
- k_bias: float32 [2048], P('tensor'), may hold values from -3 to 3
- w_value: bfloat16 [2048, 2048], P(None, 'tensor'), may hold values from -0.125 to 0.125
- v_bias: float32 [2048], P('tensor'), may hold values from -3 to 3
- w_out: bfloat16 [2048, 2048], P('tensor'), may hold values from -0.125 to 0.125
- ln2_gain: float32 [2048], replicated, may hold values from 0.5 to 1.5
- ln2_bias: float32 [2048], replicated, may hold values from -3 to 3
- w_gate: bfloat16 [2048, 3072], P(None, 'tensor'), may hold values from -0.125 to 0.125
- w_up: bfloat16 [2048, 3072], P(None, 'tensor'), may hold values from -0.125 to 0.125
- w_down: bfloat16 [3072, 2048], P('tensor'), may hold values from -0.109375 to 0.109375
- k_cache: bfloat16 [768, 128, 2048], P('seq', None, 'tensor'), may hold values from -16 to 16
- v_cache: bfloat16 [768, 128, 2048], P('seq', None, 'tensor'), may hold values from -6 to 6
Outputs:
- output: bfloat16 [4, 128, 2048], P(None, None, 'tensor')
Inputs may be any that keep to these rules, and one draw needn't show every extreme that they name: `page_table`: row b lists request b's pages in order: its first ceil(lengths[b] / 128) entries are distinct page numbers, the rest are -1; no page belongs to two requests. All pages of a request lie on one index of seq (page g on index g // 24); every index of seq uses its lowest slots, and some index uses all 24. `lengths`: 8 requests hold more than (23) * 128 positions; every other request holds at most 384.
All inputs are finite; a program needn't handle non-finite values.
Results may differ from a plain program's by a relative error of at most 0.017.
Values may be sent and summed in bfloat16 or wider, within the bound.
A program may use at most 128 MiB of HBM per device.

v0:
```python
import jax
import jax.numpy as jnp
from jax import lax
from jax.sharding import PartitionSpec as P

HD = 64
ROT = 16


EPSILON = 1e-05
NEGATIVE = -1e30
THETA = 10000.0


def rotary(field, positions, rotated):
    half_rot = rotated // 2
    frequency = THETA ** (-(jnp.arange(half_rot, dtype=jnp.float32) * 2.0) / rotated)
    angles = positions.astype(jnp.float32)[:, None] * frequency[None, :]
    cosine = jnp.concatenate([jnp.cos(angles), jnp.cos(angles)], -1)[:, None, :]
    sine_part = jnp.concatenate([jnp.sin(angles), jnp.sin(angles)], -1)[:, None, :]
    leading = field[..., :rotated]
    turned = jnp.concatenate([-leading[..., half_rot:], leading[..., :half_rot]], -1)
    return jnp.concatenate([leading * cosine + turned * sine_part, field[..., rotated:]], -1)


def norm_full(inputs, norm_gain, norm_bias):
    values = inputs.astype(jnp.float32)
    average = jnp.mean(values, -1, keepdims=True)
    squares = jnp.mean(values * values, -1, keepdims=True)
    inverse = lax.rsqrt(squares - average * average + EPSILON)
    return ((values - average) * inverse * norm_gain + norm_bias).astype(jnp.bfloat16)


def slot_owners(page_table, slot_ids):
    requests, most_pages = page_table.shape
    matched = page_table[:, :, None] == slot_ids[None, None, :]
    in_use = jnp.any(matched, axis=(0, 1))
    owners = jnp.sum(
        jnp.where(matched, jnp.arange(requests, dtype=jnp.int32)[:, None, None], 0), axis=(0, 1)
    )
    page_index = jnp.sum(
        jnp.where(matched, jnp.arange(most_pages, dtype=jnp.int32)[None, :, None], 0), axis=(0, 1)
    )
    return (in_use, owners, page_index)


def attend_pages(
    queries_req, keys_now, values_now, slot_used, slot_owner, slot_page, lengths, live_count
):
    slot_count, page_len, local_width = keys_now.shape
    requests, step_count, heads_local, head_dim = queries_req.shape
    group_size = min(slot_count, max(1, 512 // page_len))
    scale_factor = head_dim ** (-0.5)

    def one_block(block_number, running):
        first_slot = block_number * group_size
        keys_block = lax.dynamic_slice_in_dim(keys_now, first_slot, group_size, 0).reshape(
            group_size, page_len, heads_local, head_dim
        )
        values_block = lax.dynamic_slice_in_dim(values_now, first_slot, group_size, 0).reshape(
            group_size, page_len, heads_local, head_dim
        )
        block_used = lax.dynamic_slice_in_dim(slot_used, first_slot, group_size, 0)
        block_owner = lax.dynamic_slice_in_dim(slot_owner, first_slot, group_size, 0)
        block_page = lax.dynamic_slice_in_dim(slot_page, first_slot, group_size, 0)
        picked = jnp.take(queries_req, block_owner, axis=0)
        scores = (
            jnp.einsum("sqhd,sphd->sqhp", picked, keys_block, preferred_element_type=jnp.float32)
            * scale_factor
        )
        positions = block_page[:, None] * page_len + jnp.arange(page_len, dtype=jnp.int32)[None, :]
        visible = block_used[:, None] & (
            positions < jnp.take(lengths, block_owner, axis=0)[:, None]
        )
        scores = jnp.where(visible[:, None, None, :], scores, NEGATIVE)
        page_top = jnp.max(scores, -1)
        weights = jnp.where(
            visible[:, None, None, :], jnp.exp(scores - page_top[..., None]), 0.0
        ).astype(jnp.bfloat16)
        page_mass = jnp.sum(weights.astype(jnp.float32), -1)
        page_mix = jnp.einsum(
            "sqhp,sphd->sqhd", weights, values_block, preferred_element_type=jnp.float32
        )
        running_top, running_mass, running_mix = running
        onehot = (
            block_owner[:, None] == jnp.arange(requests, dtype=jnp.int32)[None, :]
        ) & block_used[:, None]
        slot_top = jnp.where(onehot[:, :, None, None], page_top[:, None], NEGATIVE)
        new_top = jnp.maximum(running_top, jnp.max(slot_top, 0))
        rescale = jnp.exp(running_top - new_top)
        slot_factor = jnp.where(
            block_used[:, None, None],
            jnp.exp(page_top - jnp.take(new_top, block_owner, axis=0)),
            0.0,
        )
        owner_rows = onehot.astype(jnp.float32)
        new_mass = running_mass * rescale + jnp.einsum(
            "sb,sqh->bqh", owner_rows, page_mass * slot_factor, precision=lax.Precision.HIGHEST
        )
        new_mix = running_mix * rescale[..., None] + jnp.einsum(
            "sb,sqhd->bqhd",
            owner_rows,
            page_mix * slot_factor[..., None],
            precision=lax.Precision.HIGHEST,
        )
        return (new_top, new_mass, new_mix)

    start_state = (
        jnp.full((requests, step_count, heads_local), NEGATIVE, jnp.float32),
        jnp.zeros((requests, step_count, heads_local), jnp.float32),
        jnp.zeros((requests, step_count, heads_local, head_dim), jnp.float32),
    )
    block_total = (live_count + group_size - 1) // group_size
    return lax.fori_loop(0, block_total, one_block, start_state)


def shards(
    tokens,
    lengths,
    page_table,
    embedding,
    ln1_gain,
    ln1_bias,
    w_query,
    q_bias,
    w_key,
    k_bias,
    w_value,
    v_bias,
    w_out,
    ln2_gain,
    ln2_bias,
    w_gate,
    w_up,
    w_down,
    k_cache,
    v_cache,
):
    step_count, requests = tokens.shape
    row_count = step_count * requests
    head_dim = HD
    heads_local = w_query.shape[1] // head_dim
    vocab_rows = embedding.shape[0]
    row_start = lax.axis_index("seq") * vocab_rows
    onehot = (
        tokens.reshape(-1)[:, None] == row_start + jnp.arange(vocab_rows, dtype=jnp.int32)[None, :]
    ).astype(jnp.bfloat16)
    looked = jnp.dot(onehot, embedding, preferred_element_type=jnp.float32)
    own_columns = lax.psum(looked.astype(jnp.bfloat16), "seq")
    residual = lax.all_gather(own_columns, "tensor", axis=1, tiled=True)
    normed = norm_full(residual, ln1_gain, ln1_bias)
    query_sum = jnp.dot(normed, w_query, preferred_element_type=jnp.float32)
    key_sum = jnp.dot(normed, w_key, preferred_element_type=jnp.float32)
    value_sum = jnp.dot(normed, w_value, preferred_element_type=jnp.float32)
    positions = (lengths[None, :] + jnp.arange(step_count, dtype=jnp.int32)[:, None]).reshape(-1)
    queries = rotary(
        (query_sum + q_bias).reshape(row_count, heads_local, head_dim), positions, ROT
    ).astype(jnp.bfloat16)
    new_keys = rotary(
        (key_sum + k_bias).reshape(row_count, heads_local, head_dim), positions, ROT
    ).astype(jnp.bfloat16)
    new_values = (value_sum + v_bias).reshape(row_count, heads_local, head_dim).astype(jnp.bfloat16)
    queries_req = queries.reshape(step_count, requests, heads_local, head_dim).transpose(1, 0, 2, 3)
    keys_req = new_keys.reshape(step_count, requests, heads_local, head_dim).transpose(1, 0, 2, 3)
    values_req = new_values.reshape(step_count, requests, heads_local, head_dim).transpose(
        1, 0, 2, 3
    )
    seq_index = lax.axis_index("seq")
    slot_count = k_cache.shape[0]
    local_slots = jnp.arange(slot_count, dtype=jnp.int32)
    slot_ids = seq_index * slot_count + local_slots
    slot_used, slot_owner, slot_page = slot_owners(page_table, slot_ids)
    live_count = jnp.sum(slot_used.astype(jnp.int32))
    running_top, running_mass, running_mix = attend_pages(
        queries_req, k_cache, v_cache, slot_used, slot_owner, slot_page, lengths, live_count
    )
    overall_page = lax.pmax(running_top, "seq")
    factor_now = jnp.exp(running_top - overall_page)
    page_mass, page_mix = (
        lax.psum((running_mass * factor_now).astype(jnp.bfloat16), "seq").astype(jnp.float32),
        lax.psum((running_mix * factor_now[..., None]).astype(jnp.bfloat16), "seq").astype(
            jnp.float32
        ),
    )
    query_sel, key_sel, value_sel = (queries_req, keys_req, values_req)
    kept_rows = step_count * requests
    scale_factor = head_dim ** (-0.5)
    causal = jnp.arange(step_count)[None, :] <= jnp.arange(step_count)[:, None]
    fresh_scores = (
        jnp.einsum("bqhd,bkhd->bqhk", query_sel, key_sel, preferred_element_type=jnp.float32)
        * scale_factor
    )
    fresh_scores = jnp.where(causal[None, :, None, :], fresh_scores, NEGATIVE)
    fresh_top = jnp.max(fresh_scores, -1)
    fresh_weights = jnp.where(
        causal[None, :, None, :], jnp.exp(fresh_scores - fresh_top[..., None]), 0.0
    ).astype(jnp.bfloat16)
    fresh_mass = jnp.sum(fresh_weights.astype(jnp.float32), -1)
    fresh_mix = jnp.einsum(
        "bqhk,bkhd->bqhd", fresh_weights, value_sel, preferred_element_type=jnp.float32
    )
    overall_top = jnp.maximum(overall_page, fresh_top)
    old_factor = jnp.exp(overall_page - overall_top)
    fresh_factor = jnp.exp(fresh_top - overall_top)
    total_mass = page_mass * old_factor + fresh_mass * fresh_factor
    total_mix = page_mix * old_factor[..., None] + fresh_mix * fresh_factor[..., None]
    attended = (total_mix / total_mass[..., None]).astype(jnp.bfloat16)
    attn_rows = attended.transpose(1, 0, 2, 3).reshape(kept_rows, heads_local * head_dim)
    attn_partial = jnp.dot(attn_rows, w_out, preferred_element_type=jnp.float32)
    attn_total = lax.psum(attn_partial.astype(jnp.bfloat16), "tensor").astype(jnp.float32)
    hidden_one = (residual.astype(jnp.float32) + attn_total).astype(jnp.bfloat16)
    normed_two = norm_full(hidden_one, ln2_gain, ln2_bias)
    gate_part = jnp.dot(normed_two, w_gate, preferred_element_type=jnp.float32)
    up_part = jnp.dot(normed_two, w_up, preferred_element_type=jnp.float32)
    activated = (jax.nn.silu(gate_part) * up_part).astype(jnp.bfloat16)
    mlp_total = lax.psum(
        jnp.dot(activated, w_down, preferred_element_type=jnp.float32).astype(jnp.bfloat16),
        "tensor",
    ).astype(jnp.float32)
    whole_output = (hidden_one.astype(jnp.float32) + mlp_total).astype(jnp.bfloat16)
    col_count = whole_output.shape[1] // lax.axis_size("tensor")
    output = lax.dynamic_slice_in_dim(
        whole_output, lax.axis_index("tensor") * col_count, col_count, 1
    )
    output = output.reshape(step_count, requests, -1)
    return output


def solution(mesh):
    placed = (
        P(),
        P(),
        P(),
        P("seq", "tensor"),
        P(),
        P(),
        P(None, "tensor"),
        P("tensor"),
        P(None, "tensor"),
        P("tensor"),
        P(None, "tensor"),
        P("tensor"),
        P("tensor", None),
        P(),
        P(),
        P(None, "tensor"),
        P(None, "tensor"),
        P("tensor", None),
        P("seq", None, "tensor"),
        P("seq", None, "tensor"),
    )
    return jax.shard_map(
        shards, mesh=mesh, in_specs=placed, out_specs=P(None, None, "tensor"), check_vma=False
    )
```

profile of v0, /device:TPU:1, one launch (start us, length us, event | category | flops | bytes accessed | tf_op | source)
XLA Modules:
  0.0 621.5 jit_solution(13988073731669611741)
XLA Ops:
  6.6 2.7 fusion.20
  9.3 146.6 %all-reduce.5.cloned.1.call-done = bf16[512,256]{1,0:T(8,128)(2,1)} async-done(((bf16[512,256]{1,0:T(8,128)(2,1)}), bf16[512,256]{1,0:T(8,128)(2,1)}) %all-reduce.5.cloned.1.call-update) | async-done | bytes 262160 | tf_op jit(solution)/shard_map/psum | solution.py:149
  156.8 0.6 convert_reduce_fusion.4
  158.3 0.6 pad_maximum_fusion
  159.2 29.8 %all-gather.2.cloned.1.call-done = bf16[512,2048]{1,0:T(8,128)(2,1)} async-done(((bf16[512,256]{1,0:T(8,128)(2,1)}), bf16[512,2048]{1,0:T(8,128)(2,1)}) %all-gather.2.cloned.1.call-update) | async-done | bytes 2097168 | tf_op jit(solution)/shard_map/all_gather | solution.py:150
  189.0 2.4 convert_reduce_fusion.1
  191.5 0.8 fusion.11
  192.8 0.8 convolution_add_fusion.2
  194.0 0.8 convolution_add_fusion.3
  194.8 0.8 slice_negate_fusion
  195.6 0.7 fusion.19
  196.5 1.2 copy.125
  197.8 1.0 fusion.42
  200.3 1.2 copy.118
  201.5 0.7 maximum_bitcast_fusion
  202.2 1.0 copy.116
  203.2 0.9 fusion.29
  204.1 0.7 copy.120
  204.8 21.5 %while.14 = (s32[]{:T(128)}, f32[128,4,4]{0,2,1:T(4,128)S(1)}, f32[128,4,4]{0,2,1:T(4,128)S(1)}, f32[128,4,4,64]{0,3,2,1:T(8,128)S(1)}, s32[]{:T(128)}, /*index=...) while((s32[]{:T(128)}, f32[128,4,4]{0,2,1:T(4,128)S(1)}, ...), condition=%wide.region_11.12_spmd, body=%wide.region_7.11_spmd.sunk | while | flops 8873650 | bytes 3987451 | solution.py:114
  205.0 0.6 gather_fusion.1
  205.7 1.6 gather_fusion
  207.4 1.1 constant_dynamic-slice_fusion.3
  211.2 0.8 convolution_add_fusion.5
  212.1 0.6 gather_fusion.1
  212.9 1.6 gather_fusion
  214.6 1.1 constant_dynamic-slice_fusion.3
  218.3 0.8 convolution_add_fusion.5
  219.3 0.6 gather_fusion.1
  220.0 1.6 gather_fusion
  221.7 1.1 constant_dynamic-slice_fusion.3
  225.5 0.8 convolution_add_fusion.5
  226.3 79.7 %pmax.7 = f32[128,4,4]{0,2,1:T(4,128)S(1)} all-reduce(f32[128,4,4]{0,2,1:T(4,128)S(1)} %get-tuple-element.71), channel_id=1, replica_groups=mesh['seq'=32,'tensor'=8] {'seq'}, use_global_device_ids=true, to_apply=%region_12.13 | all-reduce | flops 2048 | bytes 16384 | tf_op jit(solution)/shard_map/pmax | solution.py:177
  306.1 0.8 multiply_convert_fusion
  307.1 1.2 copy.126
  308.4 1.7 fusion.56
  310.6 56.6 %psum.37 = bf16[128,4,4]{0,2,1:T(4,128)(2,1)S(1)} all-reduce(bf16[128,4,4]{0,2,1:T(4,128)(2,1)S(1)} %get-tuple-element.175), channel_id=1, replica_groups=mesh['seq'=32,'tensor'=8] {'seq'}, use_global_device_ids=true, to_apply=%region_15.16 | all-reduce | flops 2048 | bytes 8192 | tf_op jit(solution)/shard_map/psum | solution.py:180
  367.1 88.1 %all-reduce.7.cloned.1.call-done = bf16[128,4,4,64]{0,3,2,1:T(8,128)(2,1)} async-done(((bf16[128,4,4,64]{0,3,2,1:T(8,128)(2,1)}), bf16[128,4,4,64]{0,3,2,1:T(8,128)(2,1)}) %all-reduce.7.cloned.1.call-update) | async-done | bytes 262160 | tf_op jit(solution)/shard_map/psum | solution.py:181
  455.2 1.1 fusion.40
  456.5 2.1 convolution_convert_fusion
  458.7 70.3 %all-reduce.9.cloned.1.call-done = bf16[512,2048]{1,0:T(8,128)(2,1)} async-done(((bf16[512,2048]{1,0:T(8,128)(2,1)}), bf16[512,2048]{1,0:T(8,128)(2,1)}) %all-reduce.9.cloned.1.call-update) | async-done | bytes 2097168 | tf_op jit(solution)/shard_map/psum | solution.py:210
  529.0 3.2 convert_reduce_fusion.2
  532.2 0.8 add_convert_fusion
  533.5 1.3 copy-done.4
  534.8 2.2 fusion.57
  537.0 5.5 convolution_convert_fusion.1
  542.5 4.1 convert_element_type.110
  546.6 66.5 %all-reduce.11.cloned.1.call-done = bf16[512,2048]{1,0:T(8,128)(2,1)} async-done(((bf16[512,2048]{1,0:T(8,128)(2,1)}), bf16[512,2048]{1,0:T(8,128)(2,1)}) %all-reduce.11.cloned.1.call-update) | async-done | bytes 2097168 | tf_op jit(solution)/shard_map/psum | solution.py:216
  613.1 1.9 fusion.28
  (156 shorter events, 14.3 us)
Async XLA Ops:
  6.5 530.5 %copy-start = (bf16[384,2048]{1,0:T(8,128)(2,1)S(1)}, bf16[384,2048]{1,0:T(8,128)(2,1)}, u32[]{:S(2)}) copy-start(bf16[384,2048]{1,0:T(8,128)(2,1)} %param.39) | copy-start | bytes 4718596
  6.5 149.5 %copy-start.9 = (s32[128,24]{0,1:T(8,128)S(1)}, s32[128,24]{0,1:T(8,128)}, u32[]{:S(2)}) copy-start(s32[128,24]{0,1:T(8,128)} %param.24) | copy-start | bytes 36868
  6.5 151.6 %copy-start.1 = (s32[128]{0:T(128)S(1)}, s32[128]{0:T(128)}, u32[]{:S(2)}) copy-start(s32[128]{0:T(128)} %param.23) | copy-start | bytes 1540
  6.5 149.4 %all-reduce.5.cloned.1.call-start = ((), (), s32[]{:S(2)}) async-start(), calls=%async_computation | async-start | bytes 524288 | tf_op jit(solution)/shard_map/psum | solution.py:149
  9.2 182.3 %copy-start.10 = (f32[2048]{0:T(1024)S(1)}, f32[2048]{0:T(1024)}, u32[]{:S(2)}) copy-start(f32[2048]{0:T(1024)} %param.27) | copy-start | bytes 24580
  9.2 182.3 %copy-start.11 = (f32[2048]{0:T(1024)S(1)}, f32[2048]{0:T(1024)}, u32[]{:S(2)}) copy-start(f32[2048]{0:T(1024)} %param.26) | copy-start | bytes 24580
  9.3 179.8 %all-gather.2.cloned.1.call-start = ((), (), s32[]{:S(2)}) async-start(), calls=%async_computation.1 | async-start | bytes 2359296 | tf_op jit(solution)/shard_map/all_gather | solution.py:150
  156.0 299.3 %all-reduce.7.cloned.1.call-start = ((), (), s32[]{:S(2)}) async-start(), calls=%async_computation.2 | async-start | bytes 524288 | tf_op jit(solution)/shard_map/psum | solution.py:181
  156.2 0.6 copy-start.14
  189.0 2.5 copy-start.3
  191.5 1.2 copy-start.18
  191.5 1.2 copy-start.21
  192.8 1.2 copy-start.19
  192.8 1.2 copy-start.22
  194.0 1.6 copy-start.20
  194.0 1.6 copy-start.23
  194.7 0.8 copy-start.8
  201.5 1.7 copy-start.5
  203.2 1.6 copy-start.15
  204.8 103.6 %copy-start.6 = (bf16[128,4,4,64]{3,1,2,0:T(4,128)(2,1)S(1)}, bf16[128,4,4,64]{3,1,2,0:T(4,128)(2,1)}, u32[]{:S(2)}) copy-start(bf16[128,4,4,64]{3,1,2,0:T(4,128)(2,1)} %copy.125) | copy-start | bytes 786436
  306.8 222.2 %all-reduce.9.cloned.1.call-start = ((), (), s32[]{:S(2)}) async-start(), calls=%async_computation.3 | async-start | bytes 4194304 | tf_op jit(solution)/shard_map/psum | solution.py:210
  310.6 146.0 %copy-start.7 = (bf16[256,2048]{1,0:T(8,128)(2,1)S(1)}, bf16[256,2048]{1,0:T(8,128)(2,1)}, u32[]{:S(2)}) copy-start(bf16[256,2048]{1,0:T(8,128)(2,1)} %param.34) | copy-start | bytes 3145732
  458.6 73.6 %copy-start.12 = (f32[2048]{0:T(1024)S(1)}, f32[2048]{0:T(1024)}, u32[]{:S(2)}) copy-start(f32[2048]{0:T(1024)} %param.36) | copy-start | bytes 24580
  458.6 73.6 %copy-start.13 = (f32[2048]{0:T(1024)S(1)}, f32[2048]{0:T(1024)}, u32[]{:S(2)}) copy-start(f32[2048]{0:T(1024)} %param.35) | copy-start | bytes 24580
  458.6 154.4 %all-reduce.11.cloned.1.call-start = ((), (), s32[]{:S(2)}) async-start(), calls=%async_computation.4 | async-start | bytes 4194304 | tf_op jit(solution)/shard_map/psum | solution.py:216
  532.2 1.3 copy-start.2
  532.2 2.6 copy-start.16
  533.5 1.3 copy-start.4
  534.8 2.2 copy-start.17
Sparse Core Ops, SparseCore 0:
  10.8 145.0 all-reduce.4
  157.8 31.2 all-gather.1
  307.0 148.2 all-reduce.6
  458.7 70.2 all-reduce.8
  542.6 70.3 all-reduce.10
where the time goes:
time: 623 us; the launch traced here: 621 us
  waiting for transfers between devices  401 us (64%)
  blocking collectives  136 us (22%)
  local copies, waits for them, and re-layouts  25.8 us (4%)
  other arithmetic  21.7 us (3%)
  matrix products  21.6 us (3%)
  between operations  14.2 us (2%)
    psum x1, waiting for transfers between devices, shards(): own_columns = lax.psum(looked.astype(jnp.bfloat16), 'seq')  147 us
    psum x1, waiting for transfers between devices, shards(): lax.psum((running_mix * factor_now[..., None]).astype(jnp.bfloat16), 'seq')  88.1 us
    pmax x1, blocking collectives, shards(): overall_page = lax.pmax(running_top, 'seq')  79.7 us
    psum x1, waiting for transfers between devices, shards(): lax.psum(attn_partial.astype(jnp.bfloat16), 'tensor').astype(jnp.float32)  70.3 us
    psum x1, waiting for transfers between devices, shards(): lax.psum(jnp.dot(activated, w_down, preferred_element_type=jnp.float32).a...  66.5 us
    psum x1, blocking collectives, shards(): lax.psum((running_mass * factor_now).astype(jnp.bfloat16), 'seq')  56.6 us
    all_gather x1, waiting for transfers between devices, shards(): residual = lax.all_gather(own_columns, 'tensor', axis=1, tiled=True)  29.8 us
  transfers between devices with their start and end apart: 5, of which 5 were waited for; matrix products, arithmetic and copies ran while one was open for 2% of the time, Pallas kernels for 0%

commit v1 on v0

v1 whole, which is shorter than its diff:
```python
import functools

import jax
import jax.numpy as jnp
from jax import lax
from jax.experimental import pallas as pl
from jax.experimental.pallas import tpu as pltpu
from jax.sharding import PartitionSpec as P

HD = 64
ROT = 16
EPSILON = 1e-05
NEGATIVE = -1e30
THETA = 10000.0
MESH = pl.DeviceIdType.MESH
F32 = jnp.float32
BF16 = jnp.bfloat16


def iota(shape, axis):
    return lax.broadcasted_iota(jnp.int32, shape, axis)


def dot(left, right):
    return jnp.dot(left, right, preferred_element_type=F32)


def dot_nt(left, right):
    return lax.dot_general(left, right, (((1,), (1,)), ((), ())), preferred_element_type=F32)


def layer_kernel(
    n_seq,
    n_ten,
    tok_ref,
    cos_ref,
    sin_ref,
    posown_ref,
    rowcol_ref,
    rowrow_ref,
    g1_ref,
    b1_ref,
    qb_ref,
    kb_ref,
    vb_ref,
    g2_ref,
    b2_ref,
    emb_hbm,
    wq_hbm,
    wk_hbm,
    wv_hbm,
    wo_hbm,
    wg_hbm,
    wu_hbm,
    wd_hbm,
    kc_hbm,
    vc_hbm,
    out_ref,
    emb,
    wq,
    wk,
    wv,
    wo,
    wg,
    wu,
    wd,
    kc,
    vc,
    send_a,
    recv_a,
    res_own,
    res_all,
    nrm,
    q_own,
    q_all,
    q_rows,
    sbuf,
    xbuf,
    send_c,
    recv_c,
    send_e,
    recv_e,
    h1_own,
    h1_all,
    send_h,
    recv_h,
    out_own,
    out_all,
    load_sem,
    send_sem,
    recv_sem,
):
    me = lax.axis_index("seq")
    mt = lax.axis_index("tensor")
    rows_own, cols = q_own.shape
    heads = cols // HD
    slots, page = kc.shape[0], kc.shape[1]
    rows_all = n_seq * rows_own
    width = n_ten * cols

    loads = []
    for index, (source, target) in enumerate(
        (
            (emb_hbm, emb),
            (wq_hbm, wq),
            (wk_hbm, wk),
            (wv_hbm, wv),
            (kc_hbm, kc),
            (vc_hbm, vc),
            (wo_hbm, wo),
            (wg_hbm, wg),
            (wu_hbm, wu),
            (wd_hbm, wd),
        )
    ):
        copy = pltpu.make_async_copy(source, target, load_sem.at[index])
        copy.start()
        loads.append(copy)

    barrier = pltpu.get_barrier_semaphore()

    @pl.loop(1, n_seq)
    def _(step):
        pl.semaphore_signal(
            barrier, inc=1, device_id=(lax.rem(me + step, n_seq), mt), device_id_type=MESH
        )

    @pl.loop(1, n_ten)
    def _(step):
        pl.semaphore_signal(
            barrier, inc=1, device_id=(me, lax.rem(mt + step, n_ten)), device_id_type=MESH
        )

    def all_to_all(stage, over_seq, source, target):
        count = n_seq if over_seq else n_ten

        @pl.loop(1, count)
        def _(step):
            if over_seq:
                peer = lax.rem(me + step, n_seq)
                device = (peer, mt)
            else:
                peer = lax.rem(mt + step, n_ten)
                device = (me, peer)
            pltpu.make_async_remote_copy(
                src_ref=source.at[peer],
                dst_ref=target.at[step - 1],
                send_sem=send_sem.at[stage],
                recv_sem=recv_sem.at[stage],
                device_id=device,
                device_id_type=MESH,
            ).start()

    def spread(stage, over_seq, source, target):
        count = n_seq if over_seq else n_ten
        own = me if over_seq else mt

        @pl.loop(1, count)
        def _(step):
            if over_seq:
                device = (lax.rem(me + step, n_seq), mt)
            else:
                device = (me, lax.rem(mt + step, n_ten))
            pltpu.make_async_remote_copy(
                src_ref=source,
                dst_ref=target.at[own],
                send_sem=send_sem.at[stage],
                recv_sem=recv_sem.at[stage],
                device_id=device,
                device_id_type=MESH,
            ).start()

    def arrived(stage, over_seq, target):
        part = target.at[pl.ds(0, (n_seq if over_seq else n_ten) - 1)]
        pltpu.make_async_copy(part, part, recv_sem.at[stage]).wait()

    def departed(stage, over_seq, target):
        part = target.at[pl.ds(0, (n_seq if over_seq else n_ten) - 1)]
        pltpu.make_async_copy(part, part, send_sem.at[stage]).wait()

    def normalise(blocks, gain, bias):
        total = jnp.zeros((rows_own, 1), F32)
        square = jnp.zeros((rows_own, 1), F32)
        for c in range(n_ten):
            part = blocks[c].astype(F32)
            total += jnp.sum(part, -1, keepdims=True)
            square += jnp.sum(part * part, -1, keepdims=True)
        average = total / width
        inverse = lax.rsqrt(square / width - average * average + EPSILON)
        for c in range(n_ten):
            at = slice(c * cols, (c + 1) * cols)
            part = blocks[c].astype(F32)
            nrm[:, at] = ((part - average) * inverse * gain[:, at] + bias[:, at]).astype(BF16)

    loads[0].wait()
    vocab = emb.shape[0]
    tile_rows = min(rows_all, 128)
    for tile in range(rows_all // tile_rows):
        at = slice(tile * tile_rows, (tile + 1) * tile_rows)
        hit = tok_ref[at, :] == iota((tile_rows, vocab), 1)
        looked = dot(jnp.where(hit, 1.0, 0.0).astype(BF16), emb[...])
        blocks = tile_rows // rows_own
        send_a[tile * blocks : (tile + 1) * blocks] = looked.astype(BF16).reshape(
            blocks, rows_own, cols
        )

    pl.semaphore_wait(barrier, n_seq + n_ten - 2)
    all_to_all(0, True, send_a, recv_a)
    own_part = send_a[me].astype(F32)
    arrived(0, True, recv_a)
    residual = own_part + jnp.sum(recv_a[...].astype(F32), 0)
    res_own[...] = residual.astype(BF16)
    spread(1, False, res_own, res_all)
    res_all[mt] = residual.astype(BF16)
    arrived(1, False, res_all)
    normalise(res_all, g1_ref, b1_ref)

    lane = iota((rows_own, cols), 1)
    first_half = (lane % HD) < (ROT // 2)

    def rotated(field):
        partner = jnp.where(
            first_half,
            pltpu.roll(field, cols - ROT // 2, 1),
            pltpu.roll(field, ROT // 2, 1),
        )
        return field * cos_ref[...] + partner * sin_ref[...]

    loads[1].wait()
    queries = rotated(dot(nrm[...], wq[...]) + qb_ref[...]).astype(BF16)
    q_own[...] = queries
    spread(2, True, q_own, q_all)
    q_all[me] = queries
    loads[2].wait()
    loads[3].wait()
    new_keys = rotated(dot(nrm[...], wk[...]) + kb_ref[...]).astype(BF16)
    new_values = (dot(nrm[...], wv[...]) + vb_ref[...]).astype(BF16)

    steps = 4
    scale = HD**-0.5
    head_of = lane // HD
    q_tall = jnp.concatenate(
        [jnp.where(head_of == h, queries, jnp.zeros_like(queries)) for h in range(heads)], 0
    )
    tall = (heads * rows_own, rows_own)
    query_row = iota(tall, 0) % rows_own
    key_row = iota(tall, 1)
    seen = (query_row // steps == key_row // steps) & (key_row <= query_row)
    fresh = jnp.where(seen, dot_nt(q_tall, new_keys) * scale, NEGATIVE)
    fresh_top = jnp.max(fresh, -1, keepdims=True)
    fresh_weights = jnp.where(seen, jnp.exp(fresh - fresh_top), 0.0).astype(BF16)
    fresh_mass = jnp.sum(fresh_weights.astype(F32), -1, keepdims=True)
    fresh_mix = dot(fresh_weights, new_values)
    top_wide = jnp.zeros((rows_own, cols), F32)
    mass_wide = jnp.zeros((rows_own, cols), F32)
    mix_wide = jnp.zeros((rows_own, cols), F32)
    for h in range(heads):
        at = slice(h * rows_own, (h + 1) * rows_own)
        top_wide = jnp.where(head_of == h, fresh_top[at], top_wide)
        mass_wide = jnp.where(head_of == h, fresh_mass[at], mass_wide)
        mix_wide = jnp.where(head_of == h, fresh_mix[at], mix_wide)

    rows_slot = slots * steps * heads
    row_code = rowcol_ref[...]
    arrived(2, True, q_all)
    pick = jnp.where(row_code == iota((rows_slot, rows_all), 1), 1.0, 0.0).astype(BF16)
    picked = dot(pick, q_all[...].reshape(rows_all, cols))
    row_head = iota((rows_slot, cols), 0) % heads
    own_head = row_head == iota((rows_slot, cols), 1) // HD
    q_rows[...] = jnp.where(own_head, picked, 0.0).astype(BF16)
    row_owner = row_code - (iota((rows_slot, 1), 0) // heads) % steps
    group = 4 if slots % 4 == 0 else 1
    span = group * page
    loads[4].wait()
    top = jnp.full((rows_slot, 1), NEGATIVE, F32)
    for g in range(slots // group):
        at = slice(g * span, (g + 1) * span)
        keys = kc[g * group : (g + 1) * group].reshape(span, cols)
        scores = dot_nt(q_rows[...], keys) * scale
        scores = jnp.where(row_owner == posown_ref[:, at], scores, NEGATIVE)
        sbuf[:, at] = scores
        top = jnp.maximum(top, jnp.max(scores, -1, keepdims=True))
    loads[5].wait()
    mass = jnp.zeros((rows_slot, 1), F32)
    mix = jnp.zeros((rows_slot, cols), F32)
    for g in range(slots // group):
        at = slice(g * span, (g + 1) * span)
        weights = jnp.exp(sbuf[:, at] - top).astype(BF16)
        mass += jnp.sum(weights.astype(F32), -1, keepdims=True)
        mix += dot(weights, vc[g * group : (g + 1) * group].reshape(span, cols))
    level = top + jnp.log(mass)
    high = level.astype(BF16).astype(F32)
    middle = (level - high).astype(BF16).astype(F32)
    low = level - high - middle
    xbuf[:, :cols] = jnp.where(own_head, mix / mass, 0.0).astype(BF16)
    extra = xbuf.shape[1] - cols
    place = iota((rows_slot, extra), 1)
    head_col = iota((rows_slot, extra), 0) % heads
    parts = jnp.where(place == head_col, high, 0.0)
    parts = jnp.where(place == head_col + heads, middle, parts)
    parts = jnp.where(place == head_col + 2 * heads, low, parts)
    xbuf[:, cols:] = parts.astype(BF16)
    put = jnp.where(rowrow_ref[...] == iota((rows_all, rows_slot), 0), 1.0, 0.0).astype(BF16)
    send_c[...] = dot(put, xbuf[...]).astype(BF16).reshape(n_seq, rows_own, cols + extra)
    all_to_all(3, True, send_c, recv_c)
    own_part = send_c[me].astype(F32)
    arrived(3, True, recv_c)
    returned = own_part + jnp.sum(recv_c[...].astype(F32), 0)
    lift = iota((extra, cols), 0)
    lift = jnp.where(
        (lift < 3 * heads) & (lift % heads == iota((extra, cols), 1) // HD), 1.0, 0.0
    ).astype(BF16)
    page_level = dot(returned[:, cols:].astype(BF16), lift)
    overall = jnp.maximum(page_level, top_wide)
    page_factor = jnp.exp(page_level - overall)
    fresh_factor = jnp.exp(top_wide - overall)
    attended = (returned[:, :cols] * page_factor + mix_wide * fresh_factor) / (
        page_factor + mass_wide * fresh_factor
    )

    loads[6].wait()
    partial = dot(attended.astype(BF16), wo[...]).astype(BF16)
    for c in range(n_ten):
        send_e[c] = partial[:, c * cols : (c + 1) * cols]
    all_to_all(4, False, send_e, recv_e)
    own_part = send_e[mt].astype(F32)
    arrived(4, False, recv_e)
    attn_total = own_part + jnp.sum(recv_e[...].astype(F32), 0)
    hidden_one = (residual + attn_total).astype(BF16)
    h1_own[...] = hidden_one
    spread(5, False, h1_own, h1_all)
    h1_all[mt] = hidden_one
    arrived(5, False, h1_all)
    normalise(h1_all, g2_ref, b2_ref)
    loads[7].wait()
    loads[8].wait()
    gate = dot(nrm[...], wg[...])
    up = dot(nrm[...], wu[...])
    activated = (gate / (1.0 + jnp.exp(-gate)) * up).astype(BF16)
    loads[9].wait()
    partial = dot(activated, wd[...]).astype(BF16)
    for c in range(n_ten):
        send_h[c] = partial[:, c * cols : (c + 1) * cols]
    all_to_all(6, False, send_h, recv_h)
    own_part = send_h[mt].astype(F32)
    arrived(6, False, recv_h)
    mlp_total = own_part + jnp.sum(recv_h[...].astype(F32), 0)
    output = (hidden_one.astype(F32) + mlp_total).astype(BF16)
    out_own[...] = output
    spread(7, True, out_own, out_all)
    out_all[me] = output
    departed(0, True, recv_a)
    departed(1, False, res_all)
    departed(2, True, q_all)
    departed(3, True, recv_c)
    departed(4, False, recv_e)
    departed(5, False, h1_all)
    departed(6, False, recv_h)
    arrived(7, True, out_all)
    out_ref[...] = out_all[...]
    departed(7, True, out_all)


def shards(
    n_seq,
    n_ten,
    tokens,
    lengths,
    page_table,
    embedding,
    ln1_gain,
    ln1_bias,
    w_query,
    q_bias,
    w_key,
    k_bias,
    w_value,
    v_bias,
    w_out,
    ln2_gain,
    ln2_bias,
    w_gate,
    w_up,
    w_down,
    k_cache,
    v_cache,
):
    steps, requests = tokens.shape
    rows_all = steps * requests
    rows_own = rows_all // n_seq
    requests_own = requests // n_seq
    slots, page, cols = k_cache.shape
    heads = cols // HD
    width = n_ten * cols
    me = lax.axis_index("seq")
    tok = (tokens - me * embedding.shape[0]).T.reshape(rows_all, 1)

    own_lengths = lax.dynamic_slice_in_dim(lengths, me * requests_own, requests_own, 0)
    positions = (own_lengths[:, None] + jnp.arange(steps, dtype=jnp.int32)[None, :]).reshape(-1)
    half_rot = ROT // 2
    frequency = THETA ** (-(jnp.arange(half_rot, dtype=F32) * 2.0) / ROT)
    angles = positions.astype(F32)[:, None] * frequency[None, :]
    cosine, sine = jnp.cos(angles), jnp.sin(angles)
    rest = HD - ROT
    cos_wide = jnp.tile(
        jnp.concatenate([cosine, cosine, jnp.ones((rows_own, rest), F32)], -1), (1, heads)
    )
    sin_wide = jnp.tile(
        jnp.concatenate([-sine, sine, jnp.zeros((rows_own, rest), F32)], -1), (1, heads)
    )

    matched = page_table[:, :, None] == me * slots + jnp.arange(slots, dtype=jnp.int32)
    request_code = jnp.arange(requests, dtype=jnp.int32)[:, None, None] * steps
    owner = jnp.sum(jnp.where(matched, request_code, 0), (0, 1))
    left = lengths[:, None] - jnp.arange(page_table.shape[1], dtype=jnp.int32) * page
    filled = jnp.sum(jnp.where(matched, jnp.clip(left, 0, page)[:, :, None], 0), (0, 1))
    leads = jnp.any(matched[:, 0], 0)
    spot = jnp.arange(page, dtype=jnp.int32)
    posown = jnp.where(spot < filled[:, None], owner[:, None], -8).reshape(1, slots * page)
    code = jnp.where(
        leads[:, None], owner[:, None] + jnp.arange(steps, dtype=jnp.int32), -1
    )
    code = jnp.broadcast_to(code[:, :, None], (slots, steps, heads)).reshape(-1)
    rows_slot = slots * steps * heads

    vmem = pl.BlockSpec(memory_space=pltpu.VMEM)
    hbm = pl.BlockSpec(memory_space=pl.ANY)
    extra = 128
    scratch = lambda *shape: pltpu.VMEM(shape, BF16)
    out = pl.pallas_call(
        functools.partial(layer_kernel, n_seq, n_ten),
        out_shape=jax.ShapeDtypeStruct((n_seq, rows_own, cols), BF16),
        in_specs=[vmem] * 13 + [hbm] * 10,
        out_specs=vmem,
        scratch_shapes=[
            scratch(*embedding.shape),
            scratch(*w_query.shape),
            scratch(*w_key.shape),
            scratch(*w_value.shape),
            scratch(*w_out.shape),
            scratch(*w_gate.shape),
            scratch(*w_up.shape),
            scratch(*w_down.shape),
            scratch(*k_cache.shape),
            scratch(*v_cache.shape),
            scratch(n_seq, rows_own, cols),
            scratch(n_seq - 1, rows_own, cols),
            scratch(rows_own, cols),
            scratch(n_ten, rows_own, cols),
            scratch(rows_own, width),
            scratch(rows_own, cols),
            scratch(n_seq, rows_own, cols),
            scratch(rows_slot, cols),
            pltpu.VMEM((rows_slot, slots * page), F32),
            scratch(rows_slot, cols + extra),
            scratch(n_seq, rows_own, cols + extra),
            scratch(n_seq - 1, rows_own, cols + extra),
            scratch(n_ten, rows_own, cols),
            scratch(n_ten - 1, rows_own, cols),
            scratch(rows_own, cols),
            scratch(n_ten, rows_own, cols),
            scratch(n_ten, rows_own, cols),
            scratch(n_ten - 1, rows_own, cols),
            scratch(rows_own, cols),
            scratch(n_seq, rows_own, cols),
            pltpu.SemaphoreType.DMA((10,)),
            pltpu.SemaphoreType.DMA((8,)),
            pltpu.SemaphoreType.DMA((8,)),
        ],
        compiler_params=pltpu.CompilerParams(
            collective_id=0, has_side_effects=True, vmem_limit_bytes=62 * 1024 * 1024
        ),
        name="layer",
    )(
        tok,
        cos_wide,
        sin_wide,
        posown,
        code[:, None],
        code[None, :],
        ln1_gain[None],
        ln1_bias[None],
        q_bias[None],
        k_bias[None],
        v_bias[None],
        ln2_gain[None],
        ln2_bias[None],
        embedding,
        w_query,
        w_key,
        w_value,
        w_out,
        w_gate,
        w_up,
        w_down,
        k_cache,
        v_cache,
    )
    out = out.reshape(requests, steps, cols)
    return out.transpose(1, 0, 2)


def solution(mesh):
    placed = (
        P(),
        P(),
        P(),
        P("seq", "tensor"),
        P(),
        P(),
        P(None, "tensor"),
        P("tensor"),
        P(None, "tensor"),
        P("tensor"),
        P(None, "tensor"),
        P("tensor"),
        P("tensor", None),
        P(),
        P(),
        P(None, "tensor"),
        P(None, "tensor"),
        P("tensor", None),
        P("seq", None, "tensor"),
        P("seq", None, "tensor"),
    )
    return jax.shard_map(
        functools.partial(shards, mesh.shape["seq"], mesh.shape["tensor"]),
        mesh=mesh,
        in_specs=placed,
        out_specs=P(None, None, "tensor"),
        check_vma=False,
    )
```

time: 623 us -> 84.4 us (0.14)
  waiting for transfers between devices: 401 us -> 0 us
  blocking collectives: 136 us -> 0 us
  Pallas kernels: 0 us -> 73.1 us
  matrix products: 21.6 us -> 0 us
  local copies, waits for them, and re-layouts: 25.8 us -> 6.59 us
  other arithmetic: 21.7 us -> 4.32 us
  between operations: 14.2 us -> 0.05 us
    psum x4 -> x0, waiting for transfers between devices: 371 us -> none  [the longest x1 147 us: shards(): own_columns = lax.psum(looked.astype(jnp.bfloat16), 'seq')]
    pmax x1 -> x0, blocking collectives: 79.7 us -> none  [shards(): overall_page = lax.pmax(running_top, 'seq')]
    pallas_call x0 -> x1, Pallas kernels: none -> 73.1 us  [shards(): pl.pallas_call(functools.partial(layer_kernel, n_seq, n_ten), out_shape=j...]
    psum x1 -> x0, blocking collectives: 56.6 us -> none  [shards(): lax.psum((running_mass * factor_now).astype(jnp.bfloat16), 'seq')]
    all_gather x1 -> x0, waiting for transfers between devices: 29.8 us -> none  [shards(): residual = lax.all_gather(own_columns, 'tensor', axis=1, tiled=True)]
    dot_general x18 -> x0, matrix products: 21.3 us -> none  [the longest x1 5.47 us: shards(): jnp.dot(activated, w_down, preferred_element_type=jnp.float32)]
    gather x9 -> x0, local copies, waits for them, and re-layouts: 8.49 us -> none  [the longest x3 4.86 us: one_block(): picked = jnp.take(queries_req, block_owner, axis=0)]
    convert_element_type x7 -> x1, other arithmetic: 8.39 us -> 0.07 us  [shards(): angles = positions.astype(F32)[:, None] * frequency[None, :]]
  transfers between devices with their start and end apart: 5 -> 0, of which waited for: 5 -> 0; matrix products, arithmetic and copies ran while one was open for 2% -> 0% of each run, Pallas kernels for 0% -> 0%
where the time goes in v1:
time: 84.4 us; the launch traced here: 84.1 us
  Pallas kernels  73.1 us (87%)
  local copies, waits for them, and re-layouts  6.59 us (8%)
  other arithmetic  4.32 us (5%)
    pallas_call x1, Pallas kernels, shards(): pl.pallas_call(functools.partial(layer_kernel, n_seq, n_ten), out_shape=j...  73.1 us
    reshape x2, local copies, waits for them, and re-layouts, shards(): out = out.reshape(requests, steps, cols)  1.75 us

profile of v1, /device:TPU:1, one launch (start us, length us, event | category | flops | bytes accessed | tf_op | source)
XLA Modules:
  0.0 84.1 jit_solution(17114301379446397900)
XLA Ops:
  0.0 0.7 dynamic_slice.3
  0.7 0.1 pad.5.clone
  0.8 0.1 pad.2.clone
  0.9 0.7 subtract_bitcast_fusion
  1.6 0.1 add_convert_fusion
  1.7 0.1 convert_element_type.11
  1.8 0.7 subtract_clamp_fusion
  2.5 0.9 %select_reduce_fusion.1 = (s32[24]{0:T(128)S(1)}, s32[24]{0:T(128)S(1)}) fusion(s32[128,24]{0,1:T(8,128)S(1)} %subtract_clamp_fusion, s32[128,24]{0,1:T(8,128)} %param.22, s32[24]{0:T(128)S(1)} %iota_add_fusion, s32[128]{0:T(128)S(1)} %iota_multiply_fusion), kind=kLoop, calls=%fused_computation.1 | loop fusion | flops 368592 | bytes 25376 | tf_op jit(solution)/shard_map/reduce_sum | solution.py:416
  3.4 0.7 fusion
  4.1 0.1 fusion.1
  4.2 0.1 maximum_maximum_fusion
  4.3 0.7 tile.9.cos_ref
  5.0 0.7 tile.21.sin_ref
  5.7 0.1 copy.29
  5.8 0.8 broadcast_compare_fusion
  6.6 0.1 slice_reduce_fusion
  6.7 0.1 add_select_fusion
  6.8 0.1 broadcast_in_dim.104
  6.9 0.7 broadcast_in_dim_reshape.7.rowrow_ref
  7.6 0.8 broadcast_in_dim_reshape.8.rowcol_ref
  8.4 0.8 reshape.156.tok_ref
  9.2 73.1 %layer.1 = bf16[32,16,256]{2,1,0:T(8,128)(2,1)} custom-call(s32[512,1]{1,0:T(8,128)} %reshape.156.tok_ref, f32[16,256]{1,0:T(8,128)} %tile.9.cos_ref, f32[16,256]{1,0:T(8,128)} %tile.21.sin_ref, s32[1,3072]{1,0:T(1,128)} %bitcast.13, s32[384,1]{1,0:T(8,128)} %broadcast_in_dim_reshape.8.rowcol_ref, s32[1,384]{1,0:T(1,128)} %broadcast_in_dim_reshape.7.rowrow_ref, ...), custom_call_target="tpu_custom_call" | custom-call | tf_op jit(solution)/shard_map/layer/pallas_call | solution.py:430
  82.3 1.0 %reshape.155 = bf16[128,4,256]{2,1,0:T(4,128)(2,1)S(1)} reshape(bf16[32,16,256]{2,1,0:T(8,128)(2,1)} %layer.1) | data formatting | bytes 524288 | tf_op jit(solution)/shard_map/reshape | solution.py:499
  83.3 0.7 copy.34
  (8 shorter events, 0.0 us)

commit v2 on v1

--- a/solution.py
+++ b/solution.py
@@ -33,11 +33,8 @@
     n_seq,
     n_ten,
     tok_ref,
-    cos_ref,
-    sin_ref,
-    posown_ref,
-    rowcol_ref,
-    rowrow_ref,
+    len_ref,
+    table_ref,
     g1_ref,
     b1_ref,
     qb_ref,
@@ -86,6 +83,10 @@
     recv_h,
     out_own,
     out_all,
+    posown,
+    pick,
+    put,
+    turn,
     load_sem,
     send_sem,
     recv_sem,
@@ -192,17 +193,108 @@
             part = blocks[c].astype(F32)
             nrm[:, at] = ((part - average) * inverse * gain[:, at] + bias[:, at]).astype(BF16)
 
+    steps, requests = tok_ref.shape
+    own_requests = rows_own // steps
+    small = jnp.concatenate(
+        [
+            tok_ref[...].astype(F32),
+            jnp.broadcast_to(len_ref[...].astype(F32), (8 - steps, requests)),
+        ],
+        0,
+    ).T
+    upper = jnp.floor(small * (1.0 / 256.0))
+    lower = (small - upper * 256.0).astype(BF16)
+    upper = upper.astype(BF16)
+
+    def expanded(selector):
+        selector = jnp.where(selector, 1.0, 0.0).astype(BF16)
+        return dot(selector, upper) * 256.0 + dot(selector, lower)
+
+    by_row = expanded(iota((rows_all, requests), 0) // steps == iota((rows_all, requests), 1))
+    step_lane = iota((rows_all, 8), 1) == iota((rows_all, 8), 0) % steps
+    token = jnp.sum(jnp.where(step_lane, by_row, 0.0), -1, keepdims=True).astype(jnp.int32)
+    token = token - me * emb.shape[0]
+
     loads[0].wait()
     vocab = emb.shape[0]
     tile_rows = min(rows_all, 128)
     for tile in range(rows_all // tile_rows):
         at = slice(tile * tile_rows, (tile + 1) * tile_rows)
-        hit = tok_ref[at, :] == iota((tile_rows, vocab), 1)
+        hit = token[at] == iota((tile_rows, vocab), 1)
         looked = dot(jnp.where(hit, 1.0, 0.0).astype(BF16), emb[...])
         blocks = tile_rows // rows_own
         send_a[tile * blocks : (tile + 1) * blocks] = looked.astype(BF16).reshape(
             blocks, rows_own, cols
         )
+
+    home_shape = (rows_own, requests)
+    home = expanded(me * own_requests + iota(home_shape, 0) // steps == iota(home_shape, 1))
+    lane = iota((rows_own, cols), 1)
+    feature = lane % HD
+    position = home[:, steps : steps + 1] + (iota((rows_own, cols), 0) % steps).astype(F32)
+    half_rot = ROT // 2
+    frequency = jnp.zeros((rows_own, cols), F32)
+    for i in range(half_rot):
+        frequency = jnp.where(feature % half_rot == i, THETA ** (-2.0 * i / ROT), frequency)
+    angle = position * frequency
+    turns = jnp.floor(angle * 0.6366197723675814 + 0.5)
+    quadrant = turns.astype(jnp.int32) % 4
+    arc = angle - turns * 1.5703125
+    arc = arc - turns * 4.837512969970703125e-4
+    arc = arc - turns * 7.54978995489188216e-8
+    arc2 = arc * arc
+    sin_arc = ((-1.9515295891e-4 * arc2 + 8.3321608736e-3) * arc2 - 1.6666654611e-1) * arc2
+    sin_arc = sin_arc * arc + arc
+    cos_arc = (2.443315711809948e-5 * arc2 - 1.388731625493765e-3) * arc2
+    cos_arc = (cos_arc + 4.166664568298827e-2) * arc2 * arc2 - 0.5 * arc2 + 1.0
+    odd = quadrant % 2 == 1
+    sine = jnp.where(odd, cos_arc, sin_arc)
+    sine = jnp.where(quadrant >= 2, -sine, sine)
+    cosine = jnp.where(odd, sin_arc, cos_arc)
+    cosine = jnp.where((quadrant == 1) | (quadrant == 2), -cosine, cosine)
+    first_half = feature < half_rot
+    cos_wide = jnp.where(feature < ROT, cosine, 1.0)
+    sin_wide = jnp.where(feature < ROT, jnp.where(first_half, -sine, sine), 0.0)
+
+    most = table_ref.shape[0]
+    table = table_ref[...].astype(F32).T.astype(jnp.int32)
+    grid = (requests, 128)
+    slot_id = me * slots + iota(grid, 1)
+    request_id = iota(grid, 0)
+    length = jnp.broadcast_to(small[:, steps : steps + 1].astype(jnp.int32), grid)
+    owner = jnp.zeros(grid, jnp.int32)
+    filled = jnp.zeros(grid, jnp.int32)
+    leads = jnp.zeros(grid, jnp.int32)
+    for j in range(most):
+        match = table[:, j : j + 1] == slot_id
+        owner = jnp.where(match, request_id, owner)
+        filled = jnp.where(match, jnp.clip(length - j * page, 0, page), filled)
+        if j == 0:
+            leads = jnp.where(match, request_id + 1, leads)
+    owner = jnp.sum(owner.astype(F32), 0, keepdims=True).astype(jnp.int32) * steps
+    filled = jnp.sum(filled.astype(F32), 0, keepdims=True).astype(jnp.int32)
+    leads = jnp.sum(leads.astype(F32), 0, keepdims=True)
+    spot = iota((1, page), 1)
+    for s in range(slots):
+        posown[:, s * page : (s + 1) * page] = jnp.where(
+            spot < filled[:, s : s + 1], owner[:, s : s + 1], -8
+        )
+    rows_slot = slots * steps * heads
+    leads = jnp.broadcast_to(leads, (8, 128)).astype(BF16)
+    per_slot = steps * heads
+    slot_of = (iota((rows_slot, 128), 0) // per_slot == iota((rows_slot, 128), 1)).astype(F32)
+    leader = dot_nt(slot_of.astype(BF16), leads)[:, :1].astype(jnp.int32)
+    row_step = (iota((rows_slot, 1), 0) // heads) % steps
+    row_code = jnp.where(leader > 0, (leader - 1) * steps + row_step, -1)
+    slot_of = (iota((128, rows_slot), 1) // per_slot == iota((128, rows_slot), 0)).astype(F32)
+    leader = dot(leads, slot_of.astype(BF16))[:1].astype(jnp.int32)
+    lane_step = (iota((1, rows_slot), 1) // heads) % steps
+    lane_code = jnp.where(leader > 0, (leader - 1) * steps + lane_step, -1)
+    pick[...] = jnp.where(row_code == iota((rows_slot, rows_all), 1), 1.0, 0.0).astype(BF16)
+    put[...] = jnp.where(lane_code == iota((rows_all, rows_slot), 0), 1.0, 0.0).astype(BF16)
+    wanted = iota((rows_all, 1), 0)
+    wanted = wanted % requests * steps + wanted // requests
+    turn[...] = jnp.where(wanted == iota((rows_all, rows_all), 1), 1.0, 0.0).astype(BF16)
 
     pl.semaphore_wait(barrier, n_seq + n_ten - 2)
     all_to_all(0, True, send_a, recv_a)
@@ -215,16 +307,13 @@
     arrived(1, False, res_all)
     normalise(res_all, g1_ref, b1_ref)
 
-    lane = iota((rows_own, cols), 1)
-    first_half = (lane % HD) < (ROT // 2)
-
     def rotated(field):
         partner = jnp.where(
             first_half,
             pltpu.roll(field, cols - ROT // 2, 1),
             pltpu.roll(field, ROT // 2, 1),
         )
-        return field * cos_ref[...] + partner * sin_ref[...]
+        return field * cos_wide + partner * sin_wide
 
     loads[1].wait()
     queries = rotated(dot(nrm[...], wq[...]) + qb_ref[...]).astype(BF16)
@@ -236,7 +325,6 @@
     new_keys = rotated(dot(nrm[...], wk[...]) + kb_ref[...]).astype(BF16)
     new_values = (dot(nrm[...], wv[...]) + vb_ref[...]).astype(BF16)
 
-    steps = 4
     scale = HD**-0.5
     head_of = lane // HD
     q_tall = jnp.concatenate(
@@ -260,15 +348,12 @@
         mass_wide = jnp.where(head_of == h, fresh_mass[at], mass_wide)
         mix_wide = jnp.where(head_of == h, fresh_mix[at], mix_wide)
 
-    rows_slot = slots * steps * heads
-    row_code = rowcol_ref[...]
     arrived(2, True, q_all)
-    pick = jnp.where(row_code == iota((rows_slot, rows_all), 1), 1.0, 0.0).astype(BF16)
-    picked = dot(pick, q_all[...].reshape(rows_all, cols))
+    picked = dot(pick[...], q_all[...].reshape(rows_all, cols))
     row_head = iota((rows_slot, cols), 0) % heads
     own_head = row_head == iota((rows_slot, cols), 1) // HD
     q_rows[...] = jnp.where(own_head, picked, 0.0).astype(BF16)
-    row_owner = row_code - (iota((rows_slot, 1), 0) // heads) % steps
+    row_owner = row_code - row_step
     group = 4 if slots % 4 == 0 else 1
     span = group * page
     loads[4].wait()
@@ -277,7 +362,7 @@
         at = slice(g * span, (g + 1) * span)
         keys = kc[g * group : (g + 1) * group].reshape(span, cols)
         scores = dot_nt(q_rows[...], keys) * scale
-        scores = jnp.where(row_owner == posown_ref[:, at], scores, NEGATIVE)
+        scores = jnp.where(row_owner == posown[:, at], scores, NEGATIVE)
         sbuf[:, at] = scores
         top = jnp.maximum(top, jnp.max(scores, -1, keepdims=True))
     loads[5].wait()
@@ -300,8 +385,7 @@
     parts = jnp.where(place == head_col + heads, middle, parts)
     parts = jnp.where(place == head_col + 2 * heads, low, parts)
     xbuf[:, cols:] = parts.astype(BF16)
-    put = jnp.where(rowrow_ref[...] == iota((rows_all, rows_slot), 0), 1.0, 0.0).astype(BF16)
-    send_c[...] = dot(put, xbuf[...]).astype(BF16).reshape(n_seq, rows_own, cols + extra)
+    send_c[...] = dot(put[...], xbuf[...]).astype(BF16).reshape(n_seq, rows_own, cols + extra)
     all_to_all(3, True, send_c, recv_c)
     own_part = send_c[me].astype(F32)
     arrived(3, True, recv_c)
@@ -357,7 +441,7 @@
     departed(5, False, h1_all)
     departed(6, False, recv_h)
     arrived(7, True, out_all)
-    out_ref[...] = out_all[...]
+    out_ref[...] = dot(turn[...], out_all[...].reshape(rows_all, cols)).astype(BF16)
     departed(7, True, out_all)
 
 
@@ -388,39 +472,9 @@
     steps, requests = tokens.shape
     rows_all = steps * requests
     rows_own = rows_all // n_seq
-    requests_own = requests // n_seq
     slots, page, cols = k_cache.shape
     heads = cols // HD
     width = n_ten * cols
-    me = lax.axis_index("seq")
-    tok = (tokens - me * embedding.shape[0]).T.reshape(rows_all, 1)
-
-    own_lengths = lax.dynamic_slice_in_dim(lengths, me * requests_own, requests_own, 0)
-    positions = (own_lengths[:, None] + jnp.arange(steps, dtype=jnp.int32)[None, :]).reshape(-1)
-    half_rot = ROT // 2
-    frequency = THETA ** (-(jnp.arange(half_rot, dtype=F32) * 2.0) / ROT)
-    angles = positions.astype(F32)[:, None] * frequency[None, :]
-    cosine, sine = jnp.cos(angles), jnp.sin(angles)
-    rest = HD - ROT
-    cos_wide = jnp.tile(
-        jnp.concatenate([cosine, cosine, jnp.ones((rows_own, rest), F32)], -1), (1, heads)
-    )
-    sin_wide = jnp.tile(
-        jnp.concatenate([-sine, sine, jnp.zeros((rows_own, rest), F32)], -1), (1, heads)
-    )
-
-    matched = page_table[:, :, None] == me * slots + jnp.arange(slots, dtype=jnp.int32)
-    request_code = jnp.arange(requests, dtype=jnp.int32)[:, None, None] * steps
-    owner = jnp.sum(jnp.where(matched, request_code, 0), (0, 1))
-    left = lengths[:, None] - jnp.arange(page_table.shape[1], dtype=jnp.int32) * page
-    filled = jnp.sum(jnp.where(matched, jnp.clip(left, 0, page)[:, :, None], 0), (0, 1))
-    leads = jnp.any(matched[:, 0], 0)
-    spot = jnp.arange(page, dtype=jnp.int32)
-    posown = jnp.where(spot < filled[:, None], owner[:, None], -8).reshape(1, slots * page)
-    code = jnp.where(
-        leads[:, None], owner[:, None] + jnp.arange(steps, dtype=jnp.int32), -1
-    )
-    code = jnp.broadcast_to(code[:, :, None], (slots, steps, heads)).reshape(-1)
     rows_slot = slots * steps * heads
 
     vmem = pl.BlockSpec(memory_space=pltpu.VMEM)
@@ -429,8 +483,8 @@
     scratch = lambda *shape: pltpu.VMEM(shape, BF16)
     out = pl.pallas_call(
         functools.partial(layer_kernel, n_seq, n_ten),
-        out_shape=jax.ShapeDtypeStruct((n_seq, rows_own, cols), BF16),
-        in_specs=[vmem] * 13 + [hbm] * 10,
+        out_shape=jax.ShapeDtypeStruct((rows_all, cols), BF16),
+        in_specs=[vmem] * 10 + [hbm] * 10,
         out_specs=vmem,
         scratch_shapes=[
             scratch(*embedding.shape),
@@ -463,6 +517,10 @@
             scratch(n_ten - 1, rows_own, cols),
             scratch(rows_own, cols),
             scratch(n_seq, rows_own, cols),
+            pltpu.VMEM((1, slots * page), jnp.int32),
+            scratch(rows_slot, rows_all),
+            scratch(rows_all, rows_slot),
+            scratch(rows_all, rows_all),
             pltpu.SemaphoreType.DMA((10,)),
             pltpu.SemaphoreType.DMA((8,)),
             pltpu.SemaphoreType.DMA((8,)),
@@ -472,12 +530,9 @@
         ),
         name="layer",
     )(
-        tok,
-        cos_wide,
-        sin_wide,
-        posown,
-        code[:, None],
-        code[None, :],
+        tokens,
+        lengths[None],
+        page_table.T,
         ln1_gain[None],
         ln1_bias[None],
         q_bias[None],
@@ -496,8 +551,7 @@
         k_cache,
         v_cache,
     )
-    out = out.reshape(requests, steps, cols)
-    return out.transpose(1, 0, 2)
+    return out.reshape(steps, requests, cols)
 
 
 def solution(mesh):

time: 84.4 us -> 74.9 us (0.89)
  local copies, waits for them, and re-layouts: 6.59 us -> 1.67 us
  other arithmetic: 4.32 us -> 0 us
    another operation x6 -> x0, local copies, waits for them, and re-layouts: 2.86 us -> none  [the longest x1 0.8 us: shards(): code[:, None]]
    reshape x3 -> x0, local copies, waits for them, and re-layouts: 2.57 us -> none  [the longest x2 1.75 us: shards(): out = out.reshape(requests, steps, cols)]
    unnamed x0 -> x1, local copies, waits for them, and re-layouts: none -> 1.67 us
    reduce_sum x1 -> x0, other arithmetic: 0.94 us -> none  [shards(): jnp.sum(jnp.where(matched, jnp.clip(left, 0, page)[:, :, None], 0), (0, 1))]
where the time goes in v2:
time: 74.9 us; the launch traced here: 74.8 us
  Pallas kernels  73.1 us (98%)
  local copies, waits for them, and re-layouts  1.67 us (2%)
    pallas_call x1, Pallas kernels, shards(): pl.pallas_call(functools.partial(layer_kernel, n_seq, n_ten), out_shape=j...  73.1 us
    unnamed x1, local copies, waits for them, and re-layouts  1.67 us

profile of v2, /device:TPU:1, one launch (start us, length us, event | category | flops | bytes accessed | tf_op | source)
XLA Modules:
  0.0 74.8 jit_solution(6978742193942414524)
XLA Ops:
  0.0 73.1 %layer.1 = bf16[512,256]{1,0:T(8,128)(2,1)} custom-call(s32[4,128]{1,0:T(4,128)} %tok_ref.1, s32[1,128]{1,0:T(1,128)} %bitcast.19, s32[24,128]{1,0:T(8,128)} %bitcast.11, f32[1,2048]{1,0:T(1,128)} %bitcast.12, f32[1,2048]{1,0:T(1,128)} %bitcast.13, f32[1,256]{1,0:T(1,128)} %bitcast.16, f32[1,256]{1,0:T(1,128)} %bitcast.17, f32[1,256]{1,0:T(1,128)} %bitcast.18, ...), custom_call_target="tpu_custom_call" | custom-call | tf_op jit(solution)/shard_map/layer/pallas_call | solution.py:484
  73.1 1.7 %copy.22 = bf16[4,128,256]{2,1,0:T(8,128)(2,1)} copy(bf16[4,128,256]{2,1,0:T(8,128)(2,1)} %bitcast.10) | data formatting | bytes 524288

commit v3 on v2

--- a/solution.py
+++ b/solution.py
@@ -132,20 +132,37 @@
             barrier, inc=1, device_id=(me, lax.rem(mt + step, n_ten)), device_id_type=MESH
         )
 
+    major, minor = (n_seq // 8, 8) if n_seq % 8 == 0 else (1, n_seq)
+
+    def far(offset, size):
+        return min(offset, size - offset)
+
+    seq_offsets = [(i, j) for i in range(major) for j in range(minor) if i or j]
+    seq_offsets.sort(
+        key=lambda o: (
+            -far(o[0], major) - far(o[1], minor),
+            far(o[0], major),
+            o[0] + o[1],
+        )
+    )
+    ten_offsets = sorted(range(1, n_ten), key=lambda o: -far(o // 2, n_ten // 2))
+
+    def partners(over_seq):
+        if over_seq:
+            for slot, (i, j) in enumerate(seq_offsets):
+                peer = lax.rem(me // minor + i, major) * minor + lax.rem(me % minor + j, minor)
+                yield slot, peer, (peer, mt)
+        else:
+            for slot, offset in enumerate(ten_offsets):
+                chip = lax.rem(mt // 2 + offset // 2, n_ten // 2)
+                peer = chip * 2 + lax.rem(mt % 2 + offset % 2, 2)
+                yield slot, peer, (me, peer)
+
     def all_to_all(stage, over_seq, source, target):
-        count = n_seq if over_seq else n_ten
-
-        @pl.loop(1, count)
-        def _(step):
-            if over_seq:
-                peer = lax.rem(me + step, n_seq)
-                device = (peer, mt)
-            else:
-                peer = lax.rem(mt + step, n_ten)
-                device = (me, peer)
+        for slot, peer, device in partners(over_seq):
             pltpu.make_async_remote_copy(
                 src_ref=source.at[peer],
-                dst_ref=target.at[step - 1],
+                dst_ref=target.at[slot],
                 send_sem=send_sem.at[stage],
                 recv_sem=recv_sem.at[stage],
                 device_id=device,
@@ -153,15 +170,8 @@
             ).start()
 
     def spread(stage, over_seq, source, target):
-        count = n_seq if over_seq else n_ten
         own = me if over_seq else mt
-
-        @pl.loop(1, count)
-        def _(step):
-            if over_seq:
-                device = (lax.rem(me + step, n_seq), mt)
-            else:
-                device = (me, lax.rem(mt + step, n_ten))
+        for slot, peer, device in partners(over_seq):
             pltpu.make_async_remote_copy(
                 src_ref=source,
                 dst_ref=target.at[own],

time: 74.9 us -> 72.3 us (0.965)
  Pallas kernels: 73.1 us -> 70.5 us
    pallas_call x1, Pallas kernels: 73.1 us -> 70.5 us  [shards(): pl.pallas_call(functools.partial(layer_kernel, n_seq, n_ten), out_shape=j...]
where the time goes in v3:
time: 72.3 us; the launch traced here: 72.1 us
  Pallas kernels  70.5 us (98%)
  local copies, waits for them, and re-layouts  1.67 us (2%)
    pallas_call x1, Pallas kernels, shards(): pl.pallas_call(functools.partial(layer_kernel, n_seq, n_ten), out_shape=j...  70.5 us
    unnamed x1, local copies, waits for them, and re-layouts  1.67 us

profile of v3, /device:TPU:1, one launch (start us, length us, event | category | flops | bytes accessed | tf_op | source)
XLA Modules:
  0.0 72.1 jit_solution(9356103753452235627)
XLA Ops:
  0.0 70.5 %layer.1 = bf16[512,256]{1,0:T(8,128)(2,1)} custom-call(s32[4,128]{1,0:T(4,128)} %tok_ref.1, s32[1,128]{1,0:T(1,128)} %bitcast.19, s32[24,128]{1,0:T(8,128)} %bitcast.11, f32[1,2048]{1,0:T(1,128)} %bitcast.12, f32[1,2048]{1,0:T(1,128)} %bitcast.13, f32[1,256]{1,0:T(1,128)} %bitcast.16, f32[1,256]{1,0:T(1,128)} %bitcast.17, f32[1,256]{1,0:T(1,128)} %bitcast.18, ...), custom_call_target="tpu_custom_call" | custom-call | tf_op jit(solution)/shard_map/layer/pallas_call | solution.py:494
  70.5 1.7 %copy.22 = bf16[4,128,256]{2,1,0:T(8,128)(2,1)} copy(bf16[4,128,256]{2,1,0:T(8,128)(2,1)} %bitcast.10) | data formatting | bytes 524288

commit v4 on v3

--- a/solution.py
+++ b/solution.py
@@ -75,6 +75,8 @@
     xbuf,
     send_c,
     recv_c,
+    send_l,
+    recv_l,
     send_e,
     recv_e,
     h1_own,
@@ -86,6 +88,7 @@
     posown,
     pick,
     put,
+    home_put,
     turn,
     load_sem,
     send_sem,
@@ -302,6 +305,9 @@
     lane_code = jnp.where(leader > 0, (leader - 1) * steps + lane_step, -1)
     pick[...] = jnp.where(row_code == iota((rows_slot, rows_all), 1), 1.0, 0.0).astype(BF16)
     put[...] = jnp.where(lane_code == iota((rows_all, rows_slot), 0), 1.0, 0.0).astype(BF16)
+    home_put[...] = jnp.where(
+        (lane_code >= 0) & (lane_code // rows_own == iota((n_seq, rows_slot), 0)), 1.0, 0.0
+    ).astype(BF16)
     wanted = iota((rows_all, 1), 0)
     wanted = wanted % requests * steps + wanted // requests
     turn[...] = jnp.where(wanted == iota((rows_all, rows_all), 1), 1.0, 0.0).astype(BF16)
@@ -387,28 +393,32 @@
     high = level.astype(BF16).astype(F32)
     middle = (level - high).astype(BF16).astype(F32)
     low = level - high - middle
-    xbuf[:, :cols] = jnp.where(own_head, mix / mass, 0.0).astype(BF16)
-    extra = xbuf.shape[1] - cols
-    place = iota((rows_slot, extra), 1)
-    head_col = iota((rows_slot, extra), 0) % heads
-    parts = jnp.where(place == head_col, high, 0.0)
-    parts = jnp.where(place == head_col + heads, middle, parts)
-    parts = jnp.where(place == head_col + 2 * heads, low, parts)
-    xbuf[:, cols:] = parts.astype(BF16)
-    send_c[...] = dot(put[...], xbuf[...]).astype(BF16).reshape(n_seq, rows_own, cols + extra)
+    place = iota((rows_slot, 128), 1)
+    here = place == (row_code % rows_own) * heads + iota((rows_slot, 128), 0) % heads
+    levels = jnp.zeros((n_seq, 128), F32)
+    for part in (high, middle, low):
+        levels += dot(home_put[...], jnp.where(here, part, 0.0).astype(BF16))
+    send_l[...] = levels.reshape(n_seq, 1, 128)
+    all_to_all(8, True, send_l, recv_l)
+    xbuf[...] = jnp.where(own_head, mix / mass, 0.0).astype(BF16)
+    send_c[...] = dot(put[...], xbuf[...]).astype(BF16).reshape(n_seq, rows_own, cols)
     all_to_all(3, True, send_c, recv_c)
+    own_level = send_l[me]
+    arrived(8, True, recv_l)
+    level_row = own_level + jnp.sum(recv_l[...], 0)
+    place = iota((rows_own, 128), 1)
+    start = iota((rows_own, 128), 0) * heads
+    page_level = jnp.zeros((rows_own, cols), F32)
+    for h in range(heads):
+        value = jnp.sum(jnp.where(place == start + h, level_row, 0.0), -1, keepdims=True)
+        page_level = jnp.where(head_of == h, value, page_level)
     own_part = send_c[me].astype(F32)
     arrived(3, True, recv_c)
     returned = own_part + jnp.sum(recv_c[...].astype(F32), 0)
-    lift = iota((extra, cols), 0)
-    lift = jnp.where(
-        (lift < 3 * heads) & (lift % heads == iota((extra, cols), 1) // HD), 1.0, 0.0
-    ).astype(BF16)
-    page_level = dot(returned[:, cols:].astype(BF16), lift)
     overall = jnp.maximum(page_level, top_wide)
     page_factor = jnp.exp(page_level - overall)
     fresh_factor = jnp.exp(top_wide - overall)
-    attended = (returned[:, :cols] * page_factor + mix_wide * fresh_factor) / (
+    attended = (returned * page_factor + mix_wide * fresh_factor) / (
         page_factor + mass_wide * fresh_factor
     )
 
@@ -447,6 +457,7 @@
     departed(1, False, res_all)
     departed(2, True, q_all)
     departed(3, True, recv_c)
+    departed(8, True, recv_l)
     departed(4, False, recv_e)
     departed(5, False, h1_all)
     departed(6, False, recv_h)
@@ -489,7 +500,6 @@
 
     vmem = pl.BlockSpec(memory_space=pltpu.VMEM)
     hbm = pl.BlockSpec(memory_space=pl.ANY)
-    extra = 128
     scratch = lambda *shape: pltpu.VMEM(shape, BF16)
     out = pl.pallas_call(
         functools.partial(layer_kernel, n_seq, n_ten),
@@ -516,9 +526,11 @@
             scratch(n_seq, rows_own, cols),
             scratch(rows_slot, cols),
             pltpu.VMEM((rows_slot, slots * page), F32),
-            scratch(rows_slot, cols + extra),
-            scratch(n_seq, rows_own, cols + extra),
-            scratch(n_seq - 1, rows_own, cols + extra),
+            scratch(rows_slot, cols),
+            scratch(n_seq, rows_own, cols),
+            scratch(n_seq - 1, rows_own, cols),
+            pltpu.VMEM((n_seq, 1, 128), F32),
+            pltpu.VMEM((n_seq - 1, 1, 128), F32),
             scratch(n_ten, rows_own, cols),
             scratch(n_ten - 1, rows_own, cols),
             scratch(rows_own, cols),
@@ -530,10 +542,11 @@
             pltpu.VMEM((1, slots * page), jnp.int32),
             scratch(rows_slot, rows_all),
             scratch(rows_all, rows_slot),
+            scratch(n_seq, rows_slot),
             scratch(rows_all, rows_all),
             pltpu.SemaphoreType.DMA((10,)),
-            pltpu.SemaphoreType.DMA((8,)),
-            pltpu.SemaphoreType.DMA((8,)),
+            pltpu.SemaphoreType.DMA((9,)),
+            pltpu.SemaphoreType.DMA((9,)),
         ],
         compiler_params=pltpu.CompilerParams(
             collective_id=0, has_side_effects=True, vmem_limit_bytes=62 * 1024 * 1024

time: 72.3 us -> 69.4 us (0.960)
  Pallas kernels: 70.5 us -> 67.5 us
    pallas_call x1, Pallas kernels: 70.5 us -> 67.5 us  [shards(): pl.pallas_call(functools.partial(layer_kernel, n_seq, n_ten), out_shape=j...]
where the time goes in v4:
time: 69.4 us; the launch traced here: 69.2 us
  Pallas kernels  67.5 us (97%)
  local copies, waits for them, and re-layouts  1.67 us (2%)
    pallas_call x1, Pallas kernels, shards(): pl.pallas_call(functools.partial(layer_kernel, n_seq, n_ten), out_shape=j...  67.5 us
    unnamed x1, local copies, waits for them, and re-layouts  1.67 us

profile of v4, /device:TPU:1, one launch (start us, length us, event | category | flops | bytes accessed | tf_op | source)
XLA Modules:
  0.0 69.2 jit_solution(2229828796660660692)
XLA Ops:
  0.0 67.5 %layer.1 = bf16[512,256]{1,0:T(8,128)(2,1)} custom-call(s32[4,128]{1,0:T(4,128)} %tok_ref.1, s32[1,128]{1,0:T(1,128)} %bitcast.19, s32[24,128]{1,0:T(8,128)} %bitcast.11, f32[1,2048]{1,0:T(1,128)} %bitcast.12, f32[1,2048]{1,0:T(1,128)} %bitcast.13, f32[1,256]{1,0:T(1,128)} %bitcast.16, f32[1,256]{1,0:T(1,128)} %bitcast.17, f32[1,256]{1,0:T(1,128)} %bitcast.18, ...), custom_call_target="tpu_custom_call" | custom-call | tf_op jit(solution)/shard_map/layer/pallas_call | solution.py:504
  67.6 1.7 %copy.22 = bf16[4,128,256]{2,1,0:T(8,128)(2,1)} copy(bf16[4,128,256]{2,1,0:T(8,128)(2,1)} %bitcast.10) | data formatting | bytes 524288
